TPU v7x, 32 devices: a whole 2x2x4 slice. The times are simulated.
32 devices in a mesh: groups: 2 (over y), rows: 4 (over z), cols: 2 (over x), sub: 2 (over core).
Axes of the slice: x: 2, y: 2, z: 4, core: 2. Of those that a mesh axis runs over, the one named last changes fastest.
Arguments:
- data_rows: bfloat16 [16384, 256], P(('groups', 'rows')), parts along dimension 0, may hold values from -6 to 6
- landmarks: bfloat16 [4096, 256], P(('groups', 'rows', 'cols')), parts along dimension 0, may hold values from -6 to 6
- factor: bfloat16 [4096, 2048], P(('groups', 'rows', 'cols'), 'sub'), parts along dimension 0, may hold values from -0.02734375 to 0.02734375
- chosen_owner: int32 [2048, 1], P('groups'), parts along dimension 0, may hold values from 0 to 3; in each aligned block of 256 rows (0 to 255, 256 to 511, ...) at most 256 rows name the same one
- chosen_local: int32 [2048], P('groups'), parts along dimension 0, may hold values from 0 to 2047
Outputs:
- leverage: float32 [16384], P(('groups', 'rows', 'cols')), parts along dimension 0
- panel: float32 [2048, 256], P(('groups', 'rows'), 'cols'), parts along dimension 0
There are 2 independent parts, one for each index of `groups`. A program takes and returns all parts, laid end to end along the dimension named above; each array names one. Nothing has to cross between parts.
Inputs may be any that keep to these rules, and one draw needn't show every extreme that they name: `chosen_owner`: in each aligned block of 256 chosen rows no owner appears more than 256 times, and in some block one owner appears exactly 256 times.
All inputs are finite; a program needn't handle non-finite values.
Results may differ from a plain program's by a relative error of at most 0.00039.
Values may be sent and summed in bfloat16 or wider, within the bound.
A program may use at most 64 MiB of HBM per device.

v0:
```python
import math
import jax
import jax.numpy as jnp
from jax import lax
from jax.sharding import PartitionSpec as P

PANEL_DEV = 64


def squared_norms(rows_in):
    return jnp.sum(jnp.square(rows_in.astype(jnp.float32)), axis=1)


def kernel_values(left, right, right_sq, rate_value, depth):
    left_sq = squared_norms(left)
    cross = lax.dot_general(
        left, right, (((1,), (1,)), ((), ())), preferred_element_type=jnp.float32
    )
    distance = left_sq[:, None] + right_sq[None, :] - 2.0 * cross
    return jnp.exp(rate_value * (2.0 * depth - distance))


def shards(data_rows, landmarks, factor, chosen_owner, chosen_local):
    slab_rows, depth = data_rows.shape
    rate_value = 0.3 / math.sqrt(8.0 * depth)
    amplitude = math.exp(2.0 * rate_value * depth)
    col_count = lax.axis_size("cols")
    sub_count = lax.axis_size("sub")
    row_count = lax.axis_size("rows")
    col_index = lax.axis_index("cols")
    sub_index = lax.axis_index("sub")
    row_index = lax.axis_index("rows")
    every_land = lax.all_gather(landmarks, ("rows", "cols"), axis=0, tiled=True)
    mixed = lax.all_to_all(factor, "cols", split_axis=1, concat_axis=0, tiled=True)
    factor_cols = lax.all_gather(mixed, "rows", axis=0, tiled=True)
    land_sq = squared_norms(every_land)
    block_rows = math.gcd(slab_rows, 256)
    blocks = data_rows.reshape(-1, block_rows, depth)

    def block_total(block):
        values = kernel_values(block, every_land, land_sq, rate_value, depth).astype(jnp.bfloat16)
        projected = jnp.dot(values, factor_cols, preferred_element_type=jnp.float32)
        return jnp.sum(projected * projected, axis=1)

    totals = lax.map(block_total, blocks).reshape(-1)
    row_totals = lax.psum_scatter(totals, "cols", scatter_dimension=0, tiled=True)
    approx = lax.psum(row_totals, "sub")
    leverage = (amplitude - approx) / 8.0
    block_owners = chosen_owner[:, 0].reshape(row_count, -1)
    local_rows = chosen_local.reshape(row_count, -1)
    chosen_dev = block_owners.shape[1]
    capacity = 8 * max(1, chosen_dev // (2 * row_count))
    mine_mask = (block_owners == row_index).astype(jnp.int32)
    slot_rank = jnp.cumsum(mine_mask, axis=1) - mine_mask
    replicas = col_count * sub_count
    share_size = capacity // replicas
    replica_index = col_index * sub_count + sub_index
    slot_ids = replica_index * share_size + jnp.arange(share_size, dtype=jnp.int32)
    picked = (mine_mask[:, None, :] == 1) & (slot_rank[:, None, :] == slot_ids[None, :, None])
    source = jnp.sum(jnp.where(picked, local_rows[:, None, :], 0), axis=2)
    filled = jnp.any(picked, axis=2)
    picked_rows = jnp.take(data_rows, source.reshape(-1), axis=0).reshape(
        row_count, share_size, depth
    )
    outgoing = jnp.where(filled[:, :, None], picked_rows, jnp.zeros((), jnp.bfloat16))
    moved = lax.all_to_all(outgoing, "rows", split_axis=0, concat_axis=0, tiled=True)
    arrived = lax.all_gather(moved, ("cols", "sub"), axis=1, tiled=True)
    block_owner = lax.dynamic_index_in_dim(block_owners, row_index, 0, keepdims=False)
    before = jnp.tril(jnp.ones((chosen_dev, chosen_dev), jnp.bool_), -1)
    matched = (block_owner[:, None] == block_owner[None, :]) & before
    own_rank = jnp.sum(matched.astype(jnp.int32), axis=1)
    flattened = arrived.reshape(row_count * capacity, depth)
    chosen_rows = jnp.take(flattened, block_owner * capacity + own_rank, axis=0)
    per_block = PANEL_DEV // col_count
    piece = lax.dynamic_slice_in_dim(chosen_rows, col_index * per_block, per_block, 0)
    column_rows = lax.all_gather(piece, "rows", axis=0, tiled=True)
    panel = kernel_values(chosen_rows, column_rows, squared_norms(column_rows), rate_value, depth)
    return (leverage, panel)


def solution(mesh):
    placed = (
        P(("groups", "rows"), None),
        P(("groups", "rows", "cols"), None),
        P(("groups", "rows", "cols"), "sub"),
        P("groups", None),
        P("groups"),
    )
    return jax.shard_map(
        shards,
        mesh=mesh,
        in_specs=placed,
        out_specs=(P(("groups", "rows", "cols")), P(("groups", "rows"), "cols")),
        check_vma=False,
    )
```

profile of v0, /device:TPU:0, one launch (start us, length us, event | category | flops | bytes accessed | tf_op | source)
XLA Modules:
  0.0 143.4 jit_solution(4056909570043862323)
XLA Ops:
  7.2 0.7 all-gather.3.cloned.1.call-update
  7.9 1.9 %copy.21 = bf16[32,2,8,512]{3,2,0,1:T(8,128)(2,1)} copy(bf16[32,2,8,512]{3,2,1,0:T(8,128)(2,1)} %bitcast.51) | data formatting | bytes 1048576 | tf_op jit(solution)/shard_map/all_to_all | solution.py:34
  9.8 4.2 %all-to-all-start = ((bf16[256,2,512]{2,0,1:T(8,128)(2,1)}), bf16[256,2,512]{2,0,1:T(8,128)(2,1)S(1)}, u32[]{:S(2)}, u32[]{:S(2)}) async-start(bf16[256,2,512]{2,0,1:T(8,128)(2,1)} %bitcast.37), calls=%async_computation | async-start | bytes 1048576 | tf_op jit(solution)/shard_map/all_to_all | solution.py:34
  14.1 0.5 broadcast.128
  14.6 0.7 reduce.3
  15.3 1.2 reduce-window.6
  16.9 5.9 %all-to-all-done = bf16[256,2,512]{2,0,1:T(8,128)(2,1)S(1)} async-done(((bf16[256,2,512]{2,0,1:T(8,128)(2,1)}), bf16[256,2,512]{2,0,1:T(8,128)(2,1)S(1)}, u32[]{:S(2)}, u32[]{:S(2)}) %all-to-all-start) | async-done | bytes 524320 | tf_op jit(solution)/shard_map/all_to_all | solution.py:34
  22.8 0.8 copy-done.1
  23.6 0.2 select_reduce_fusion
  24.0 1.2 gather_fusion
  25.4 0.8 select_select_fusion
  26.2 5.1 %all-to-all-start.1 = ((bf16[4,64,256]{2,1,0:T(8,128)(2,1)}), bf16[4,64,256]{2,1,0:T(8,128)(2,1)S(1)}, u32[]{:S(2)}, u32[]{:S(2)}) async-start(bf16[4,64,256]{2,1,0:T(8,128)(2,1)} %select_select_fusion), calls=%async_computation.1 | async-start | bytes 262144 | tf_op jit(solution)/shard_map/all_to_all | solution.py:66
  31.3 0.6 dynamic-slice
  32.7 4.5 %all-to-all-done.1 = bf16[4,64,256]{2,1,0:T(8,128)(2,1)S(1)} async-done(((bf16[4,64,256]{2,1,0:T(8,128)(2,1)}), bf16[4,64,256]{2,1,0:T(8,128)(2,1)S(1)}, u32[]{:S(2)}, u32[]{:S(2)}) %all-to-all-start.1) | async-done | bytes 131104 | tf_op jit(solution)/shard_map/all_to_all | solution.py:66
  37.2 9.6 %all_gather.14 = bf16[4,256,256]{2,1,0:T(8,128)(2,1)S(1)} all-gather(bf16[4,64,256]{2,1,0:T(8,128)(2,1)S(1)} %all-to-all-done.1), channel_id=1, replica_groups=mesh['groups'=2,'rows'=4,'cols'=2,'sub'=2] {'cols','sub'}, dimensions={1}, use_global_device_ids=true | all-gather | bytes 655360 | tf_op jit(solution)/shard_map/all_gather | solution.py:67
  46.8 1.1 gather_fusion.1
  48.2 13.2 %all_gather.15 = bf16[128,256]{1,0:T(8,128)(2,1)S(1)} all-gather(bf16[32,256]{1,0:T(8,128)(2,1)S(1)} %constant_dynamic-slice_fusion), channel_id=1, replica_groups=mesh['groups'=2,'rows'=4,'cols'=2,'sub'=2] {'rows'}, dimensions={0}, use_global_device_ids=true | all-gather | bytes 81920 | tf_op jit(solution)/shard_map/all_gather | solution.py:76
  61.5 0.9 fusion.18
  62.4 1.6 %multiply_reduce_fusion.1 = f32[2048]{0:T(1024)S(1)} fusion(bf16[2048,256]{1,0:T(8,128)(2,1)} %all-gather.3.cloned.1.call-done), kind=kLoop, calls=%fused_computation.17 | loop fusion | flops 1570816 | bytes 1056768 | tf_op jit(solution)/shard_map/reduce_sum | solution.py:11
  64.0 36.9 %all-gather.5.cloned.1.call-done = bf16[2048,512]{1,0:T(8,128)(2,1)} async-done(((bf16[512,512]{1,0:T(8,128)(2,1)}), bf16[2048,512]{1,0:T(8,128)(2,1)}) %all-gather.5.cloned.1.call-update) | async-done | bytes 2097168 | tf_op jit(solution)/shard_map/all_gather | solution.py:35
  100.9 27.6 %while.10 = (s32[]{:T(128)}, f32[8,256]{1,0:T(8,128)S(1)}, bf16[8,256,256]{2,1,0:T(8,128)(2,1)S(1)}, f32[2048]{0:T(1024)S(1)}, bf16[2048,256]{1,0:T(8,128)(2,1)}...) while((s32[]{:T(128)}, f32[8,256]{1,0:T(8,128)S(1)}, bf16[8,256,256]{2,1,0:T(8,128)(2,1)S(1)}, ...), condition=%wide.region_4.5_spmd, body=%wide.region_1.4_spmd.sunk | while | flops 808910336 | bytes 3421289 | solution.py:45
  101.0 3.3 %fusion.32 = f32[256]{0:T(256)S(1)} fusion(bf16[2048,512]{1,0:T(8,128)(2,1)} %get-tuple-element.109, bf16[2048,256]{1,0:T(8,128)(2,1)} %get-tuple-element.108, f32[2048]{0:T(1024)S(1)} %get-tuple-element.107, f32[256]{0:T(256)S(1)} %multiply_reduce_fusion.5, bf16[8,256,256]{2,1,0:T(8,128)(2,1)S(1)} %get-tuple-element.106, s32[]{:T(128)S(6)} %copy.25), kind=kOutput, calls=%fused_computation.9.clone.1 | convolution fusion | flops 808713984 | bytes 3287044 | tf_op jit(solution)/shard_map/while/body/eval_jaxpr/dot_general | solution.py:42
  104.5 3.3 %fusion.32 = f32[256]{0:T(256)S(1)} fusion(bf16[2048,512]{1,0:T(8,128)(2,1)} %get-tuple-element.109, bf16[2048,256]{1,0:T(8,128)(2,1)} %get-tuple-element.108, f32[2048]{0:T(1024)S(1)} %get-tuple-element.107, f32[256]{0:T(256)S(1)} %multiply_reduce_fusion.5, bf16[8,256,256]{2,1,0:T(8,128)(2,1)S(1)} %get-tuple-element.106, s32[]{:T(128)S(6)} %copy.25), kind=kOutput, calls=%fused_computation.9.clone.1 | convolution fusion | flops 808713984 | bytes 3287044 | tf_op jit(solution)/shard_map/while/body/eval_jaxpr/dot_general | solution.py:42
  107.9 3.3 %fusion.32 = f32[256]{0:T(256)S(1)} fusion(bf16[2048,512]{1,0:T(8,128)(2,1)} %get-tuple-element.109, bf16[2048,256]{1,0:T(8,128)(2,1)} %get-tuple-element.108, f32[2048]{0:T(1024)S(1)} %get-tuple-element.107, f32[256]{0:T(256)S(1)} %multiply_reduce_fusion.5, bf16[8,256,256]{2,1,0:T(8,128)(2,1)S(1)} %get-tuple-element.106, s32[]{:T(128)S(6)} %copy.25), kind=kOutput, calls=%fused_computation.9.clone.1 | convolution fusion | flops 808713984 | bytes 3287044 | tf_op jit(solution)/shard_map/while/body/eval_jaxpr/dot_general | solution.py:42
  111.4 3.3 %fusion.32 = f32[256]{0:T(256)S(1)} fusion(bf16[2048,512]{1,0:T(8,128)(2,1)} %get-tuple-element.109, bf16[2048,256]{1,0:T(8,128)(2,1)} %get-tuple-element.108, f32[2048]{0:T(1024)S(1)} %get-tuple-element.107, f32[256]{0:T(256)S(1)} %multiply_reduce_fusion.5, bf16[8,256,256]{2,1,0:T(8,128)(2,1)S(1)} %get-tuple-element.106, s32[]{:T(128)S(6)} %copy.25), kind=kOutput, calls=%fused_computation.9.clone.1 | convolution fusion | flops 808713984 | bytes 3287044 | tf_op jit(solution)/shard_map/while/body/eval_jaxpr/dot_general | solution.py:42
  114.8 3.3 %fusion.32 = f32[256]{0:T(256)S(1)} fusion(bf16[2048,512]{1,0:T(8,128)(2,1)} %get-tuple-element.109, bf16[2048,256]{1,0:T(8,128)(2,1)} %get-tuple-element.108, f32[2048]{0:T(1024)S(1)} %get-tuple-element.107, f32[256]{0:T(256)S(1)} %multiply_reduce_fusion.5, bf16[8,256,256]{2,1,0:T(8,128)(2,1)S(1)} %get-tuple-element.106, s32[]{:T(128)S(6)} %copy.25), kind=kOutput, calls=%fused_computation.9.clone.1 | convolution fusion | flops 808713984 | bytes 3287044 | tf_op jit(solution)/shard_map/while/body/eval_jaxpr/dot_general | solution.py:42
  118.3 3.3 %fusion.32 = f32[256]{0:T(256)S(1)} fusion(bf16[2048,512]{1,0:T(8,128)(2,1)} %get-tuple-element.109, bf16[2048,256]{1,0:T(8,128)(2,1)} %get-tuple-element.108, f32[2048]{0:T(1024)S(1)} %get-tuple-element.107, f32[256]{0:T(256)S(1)} %multiply_reduce_fusion.5, bf16[8,256,256]{2,1,0:T(8,128)(2,1)S(1)} %get-tuple-element.106, s32[]{:T(128)S(6)} %copy.25), kind=kOutput, calls=%fused_computation.9.clone.1 | convolution fusion | flops 808713984 | bytes 3287044 | tf_op jit(solution)/shard_map/while/body/eval_jaxpr/dot_general | solution.py:42
  121.7 3.3 %fusion.32 = f32[256]{0:T(256)S(1)} fusion(bf16[2048,512]{1,0:T(8,128)(2,1)} %get-tuple-element.109, bf16[2048,256]{1,0:T(8,128)(2,1)} %get-tuple-element.108, f32[2048]{0:T(1024)S(1)} %get-tuple-element.107, f32[256]{0:T(256)S(1)} %multiply_reduce_fusion.5, bf16[8,256,256]{2,1,0:T(8,128)(2,1)S(1)} %get-tuple-element.106, s32[]{:T(128)S(6)} %copy.25), kind=kOutput, calls=%fused_computation.9.clone.1 | convolution fusion | flops 808713984 | bytes 3287044 | tf_op jit(solution)/shard_map/while/body/eval_jaxpr/dot_general | solution.py:42
  125.2 3.3 %fusion.32 = f32[256]{0:T(256)S(1)} fusion(bf16[2048,512]{1,0:T(8,128)(2,1)} %get-tuple-element.109, bf16[2048,256]{1,0:T(8,128)(2,1)} %get-tuple-element.108, f32[2048]{0:T(1024)S(1)} %get-tuple-element.107, f32[256]{0:T(256)S(1)} %multiply_reduce_fusion.5, bf16[8,256,256]{2,1,0:T(8,128)(2,1)S(1)} %get-tuple-element.106, s32[]{:T(128)S(6)} %copy.25), kind=kOutput, calls=%fused_computation.9.clone.1 | convolution fusion | flops 808713984 | bytes 3287044 | tf_op jit(solution)/shard_map/while/body/eval_jaxpr/dot_general | solution.py:42
  128.5 5.0 %all-reduce = f32[2048]{0:T(1024)S(1)} all-reduce(f32[2048]{0:T(1024)S(1)} %bitcast.53), channel_id=2, replica_groups=mesh['groups'=2,'rows'=4,'cols'=2,'sub'=2] {'cols'}, use_global_device_ids=true, to_apply=%region_5.6.clone | all-reduce | flops 2048 | bytes 16384
  133.5 2.5 %psum.7 = f32[1024]{0:T(1024)S(1)} all-reduce(f32[1024]{0:T(1024)S(1)} %dynamic-slice.1), channel_id=1, replica_groups=mesh['groups'=2,'rows'=4,'cols'=2,'sub'=2] {'sub'}, use_global_device_ids=true, to_apply=%region_6.7 | all-reduce | flops 1024 | bytes 8192 | tf_op jit(solution)/shard_map/psum | solution.py:47
  136.0 0.6 subtract_multiply_fusion
  (58 shorter events, 2.7 us)
Async XLA Ops:
  7.2 7.4 %copy-start.2 = (s32[1024,1]{0,1:T(1,128)S(1)}, s32[1024,1]{0,1:T(1,128)}, u32[]{:S(2)}) copy-start(s32[1024,1]{0,1:T(1,128)} %param.10) | copy-start | bytes 12292
  7.2 16.4 %copy-start.3 = (s32[1024]{0:T(1024)S(1)}, s32[1024]{0:T(1024)}, u32[]{:S(2)}) copy-start(s32[1024]{0:T(1024)} %param.11) | copy-start | bytes 12292
  7.2 16.8 %copy-start = (bf16[2048,256]{1,0:T(8,128)(2,1)S(1)}, bf16[2048,256]{1,0:T(8,128)(2,1)}, u32[]{:S(2)}) copy-start(bf16[2048,256]{1,0:T(8,128)(2,1)} %param.7) | copy-start | bytes 3145732
  7.2 55.2 %all-gather.3.cloned.1.call-start = ((), (), s32[]{:S(2)}) async-start(), calls=%async_computation.2 | async-start | bytes 1179648 | tf_op jit(solution)/shard_map/all_gather | solution.py:33
  7.9 23.4 %copy-start.4 = (u32[32]{0:T(128)S(1)}, u32[32]{0:T(128)}, u32[]{:S(2)}) copy-start(u32[32]{0:T(128)} %constant.104) | copy-start | bytes 388
  9.8 13.0 %all-to-all-start = ((bf16[256,2,512]{2,0,1:T(8,128)(2,1)}), bf16[256,2,512]{2,0,1:T(8,128)(2,1)S(1)}, u32[]{:S(2)}, u32[]{:S(2)}) async-start(bf16[256,2,512]{2,0,1:T(8,128)(2,1)} %bitcast.37), calls=%async_computation | async-start | bytes 1048576 | tf_op jit(solution)/shard_map/all_to_all | solution.py:34
  14.0 86.8 %all-gather.5.cloned.1.call-start = ((), (), s32[]{:S(2)}) async-start(), calls=%async_computation.3 | async-start | bytes 2621440 | tf_op jit(solution)/shard_map/all_gather | solution.py:35
  22.8 0.8 copy-start.1
  26.2 11.0 %all-to-all-start.1 = ((bf16[4,64,256]{2,1,0:T(8,128)(2,1)}), bf16[4,64,256]{2,1,0:T(8,128)(2,1)S(1)}, u32[]{:S(2)}, u32[]{:S(2)}) async-start(bf16[4,64,256]{2,1,0:T(8,128)(2,1)} %select_select_fusion), calls=%async_computation.1 | async-start | bytes 262144 | tf_op jit(solution)/shard_map/all_to_all | solution.py:66
Sparse Core Ops, SparseCore 0:
  10.1 44.1 all-gather.2
  55.9 44.9 all-gather.4
where the time goes:
time: 144 us; the launch traced here: 143 us
  waiting for transfers between devices  47.9 us (33%)
  blocking collectives  30.3 us (21%)
  matrix products  27 us (19%)
  between operations  14.8 us (10%)
  starting transfers between devices  9.39 us (7%)
  other arithmetic  6.97 us (5%)
  local copies, waits for them, and re-layouts  6.81 us (5%)
    all_gather x1, waiting for transfers between devices, shards(): factor_cols = lax.all_gather(mixed, 'rows', axis=0, tiled=True)  36.9 us
    dot_general x8, matrix products, block_total(): projected = jnp.dot(values, factor_cols, preferred_element_type=jnp.float32)  26.1 us
    all_gather x1, blocking collectives, shards(): column_rows = lax.all_gather(piece, 'rows', axis=0, tiled=True)  13.2 us
    all_gather x1, blocking collectives, shards(): arrived = lax.all_gather(moved, ('cols', 'sub'), axis=1, tiled=True)  9.63 us
    all_to_all x1, waiting for transfers between devices, shards(): lax.all_to_all(factor, 'cols', split_axis=1, concat_axis=0, tiled=True)  5.88 us
    all_to_all x1, starting transfers between devices, shards(): lax.all_to_all(outgoing, 'rows', split_axis=0, concat_axis=0, tiled=True)  5.12 us
    unnamed x1, blocking collectives  5 us
    all_to_all x1, waiting for transfers between devices, shards(): lax.all_to_all(outgoing, 'rows', split_axis=0, concat_axis=0, tiled=True)  4.48 us
  transfers between devices with their start and end apart: 4, of which 3 were waited for; matrix products, arithmetic and copies ran while one was open for 8% of the time, Pallas kernels for 0%

commit v1 on v0

--- a/solution.py
+++ b/solution.py
@@ -73,7 +73,12 @@
     chosen_rows = jnp.take(flattened, block_owner * capacity + own_rank, axis=0)
     per_block = PANEL_DEV // col_count
     piece = lax.dynamic_slice_in_dim(chosen_rows, col_index * per_block, per_block, 0)
-    column_rows = lax.all_gather(piece, "rows", axis=0, tiled=True)
+    ring = [piece]
+    for hop in range(3):
+        ring.append(lax.ppermute(ring[-1], "rows", [(dev, (dev + 1) % 4) for dev in range(4)]))
+    column_rows = jnp.roll(
+        jnp.concatenate(ring[::-1], axis=0), (lax.axis_index("rows") + 1) * ring[0].shape[0], axis=0
+    )
     panel = kernel_values(chosen_rows, column_rows, squared_norms(column_rows), rate_value, depth)
     return (leverage, panel)
 

time: 144 us -> 145 us (level)
  blocking collectives: 30.3 us -> 17.1 us
  waiting for transfers between devices: 47.9 us -> 60.6 us
    ppermute x0 -> x3, waiting for transfers between devices: none -> 14.5 us  [shards(): lax.ppermute(ring[-1], 'rows', [(dev, (dev + 1) % 4) for dev in range(4)])]
    all_gather x1 -> x0, blocking collectives: 13.2 us -> none  [shards(): column_rows = lax.all_gather(piece, 'rows', axis=0, tiled=True)]
    all_gather x1, waiting for transfers between devices: 36.9 us -> 33.9 us  [shards(): factor_cols = lax.all_gather(mixed, 'rows', axis=0, tiled=True)]
  transfers between devices with their start and end apart: 4 -> 7, of which waited for: 3 -> 6; matrix products, arithmetic and copies ran while one was open for 8% -> 8% of each run, Pallas kernels for 0% -> 0%
where the time goes in v1:
time: 145 us; the launch traced here: 144 us
  waiting for transfers between devices  60.6 us (42%)
  matrix products  27 us (19%)
  blocking collectives  17.1 us (12%)
  between operations  14.9 us (10%)
  starting transfers between devices  10.5 us (7%)
  other arithmetic  6.91 us (5%)
  local copies, waits for them, and re-layouts  6.85 us (5%)
    all_gather x1, waiting for transfers between devices, shards(): factor_cols = lax.all_gather(mixed, 'rows', axis=0, tiled=True)  33.9 us
    dot_general x8, matrix products, block_total(): projected = jnp.dot(values, factor_cols, preferred_element_type=jnp.float32)  26.1 us
    ppermute x3, waiting for transfers between devices, shards(): lax.ppermute(ring[-1], 'rows', [(dev, (dev + 1) % 4) for dev in range(4)])  14.5 us
    all_gather x1, blocking collectives, shards(): arrived = lax.all_gather(moved, ('cols', 'sub'), axis=1, tiled=True)  9.58 us
    all_to_all x1, waiting for transfers between devices, shards(): lax.all_to_all(outgoing, 'rows', split_axis=0, concat_axis=0, tiled=True)  5.9 us
    all_to_all x1, waiting for transfers between devices, shards(): lax.all_to_all(factor, 'cols', split_axis=1, concat_axis=0, tiled=True)  5.61 us
    all_to_all x1, starting transfers between devices, shards(): lax.all_to_all(outgoing, 'rows', split_axis=0, concat_axis=0, tiled=True)  5.12 us
    unnamed x1, blocking collectives  5 us
  transfers between devices with their start and end apart: 7, of which 6 were waited for; matrix products, arithmetic and copies ran while one was open for 8% of the time, Pallas kernels for 0%

profile of v1, /device:TPU:0, one launch (start us, length us, event | category | flops | bytes accessed | tf_op | source)
XLA Modules:
  0.0 144.0 jit_solution(8793351542890969113)
XLA Ops:
  7.2 0.7 all-gather.3.cloned.1.call-update
  7.9 1.9 %copy.21 = bf16[32,2,8,512]{3,2,0,1:T(8,128)(2,1)} copy(bf16[32,2,8,512]{3,2,1,0:T(8,128)(2,1)} %bitcast.50) | data formatting | bytes 1048576 | tf_op jit(solution)/shard_map/all_to_all | solution.py:34
  9.8 4.2 %all-to-all-start = ((bf16[256,2,512]{2,0,1:T(8,128)(2,1)}), bf16[256,2,512]{2,0,1:T(8,128)(2,1)S(1)}, u32[]{:S(2)}, u32[]{:S(2)}) async-start(bf16[256,2,512]{2,0,1:T(8,128)(2,1)} %bitcast.36), calls=%async_computation | async-start | bytes 1048576 | tf_op jit(solution)/shard_map/all_to_all | solution.py:34
  14.5 0.7 reduce.3
  15.2 1.2 reduce-window.6
  17.1 5.6 %all-to-all-done = bf16[256,2,512]{2,0,1:T(8,128)(2,1)S(1)} async-done(((bf16[256,2,512]{2,0,1:T(8,128)(2,1)}), bf16[256,2,512]{2,0,1:T(8,128)(2,1)S(1)}, u32[]{:S(2)}, u32[]{:S(2)}) %all-to-all-start) | async-done | bytes 524320 | tf_op jit(solution)/shard_map/all_to_all | solution.py:34
  22.8 0.8 copy-done.1
  23.9 1.2 gather_fusion
  25.3 0.8 select_select_fusion
  26.1 5.1 %all-to-all-start.1 = ((bf16[4,64,256]{2,1,0:T(8,128)(2,1)}), bf16[4,64,256]{2,1,0:T(8,128)(2,1)S(1)}, u32[]{:S(2)}, u32[]{:S(2)}) async-start(bf16[4,64,256]{2,1,0:T(8,128)(2,1)} %select_select_fusion), calls=%async_computation.1 | async-start | bytes 262144 | tf_op jit(solution)/shard_map/all_to_all | solution.py:66
  31.2 5.9 %all-to-all-done.1 = bf16[4,64,256]{2,1,0:T(8,128)(2,1)S(1)} async-done(((bf16[4,64,256]{2,1,0:T(8,128)(2,1)}), bf16[4,64,256]{2,1,0:T(8,128)(2,1)S(1)}, u32[]{:S(2)}, u32[]{:S(2)}) %all-to-all-start.1) | async-done | bytes 131104 | tf_op jit(solution)/shard_map/all_to_all | solution.py:66
  37.1 9.6 %all_gather.11 = bf16[4,256,256]{2,1,0:T(8,128)(2,1)S(1)} all-gather(bf16[4,64,256]{2,1,0:T(8,128)(2,1)S(1)} %all-to-all-done.1), channel_id=1, replica_groups=mesh['groups'=2,'rows'=4,'cols'=2,'sub'=2] {'cols','sub'}, dimensions={1}, use_global_device_ids=true | all-gather | bytes 655360 | tf_op jit(solution)/shard_map/all_gather | solution.py:67
  46.7 1.1 gather_fusion.1
  48.1 1.1 collective-permute-start
  49.2 4.7 %collective-permute-done = bf16[32,256]{1,0:T(8,128)(2,1)S(1)} collective-permute-done((bf16[32,256]{1,0:T(8,128)(2,1)S(1)}, bf16[32,256]{1,0:T(8,128)(2,1)S(1)}, u32[]{:S(2)}, u32[]{:S(2)}) %collective-permute-start) | collective-permute-done | bytes 16416 | tf_op jit(solution)/shard_map/ppermute | solution.py:78
  53.9 5.5 %collective-permute-done.1 = bf16[32,256]{1,0:T(8,128)(2,1)S(1)} collective-permute-done((bf16[32,256]{1,0:T(8,128)(2,1)S(1)}, bf16[32,256]{1,0:T(8,128)(2,1)S(1)}, u32[]{:S(2)}, u32[]{:S(2)}) %collective-permute-start.1) | collective-permute-done | bytes 16416 | tf_op jit(solution)/shard_map/ppermute | solution.py:78
  60.7 4.3 %collective-permute-done.2 = bf16[32,256]{1,0:T(8,128)(2,1)S(1)} collective-permute-done((bf16[32,256]{1,0:T(8,128)(2,1)S(1)}, bf16[32,256]{1,0:T(8,128)(2,1)S(1)}, u32[]{:S(2)}, u32[]{:S(2)}) %collective-permute-start.2) | collective-permute-done | bytes 16416 | tf_op jit(solution)/shard_map/ppermute | solution.py:78
  65.2 0.9 fusion.18
  66.0 1.6 %multiply_reduce_fusion.1 = f32[2048]{0:T(1024)S(1)} fusion(bf16[2048,256]{1,0:T(8,128)(2,1)} %all-gather.3.cloned.1.call-done), kind=kLoop, calls=%fused_computation.17 | loop fusion | flops 1570816 | bytes 1056768 | tf_op jit(solution)/shard_map/reduce_sum | solution.py:11
  67.6 33.9 %all-gather.5.cloned.1.call-done = bf16[2048,512]{1,0:T(8,128)(2,1)} async-done(((bf16[512,512]{1,0:T(8,128)(2,1)}), bf16[2048,512]{1,0:T(8,128)(2,1)}) %all-gather.5.cloned.1.call-update) | async-done | bytes 2097168 | tf_op jit(solution)/shard_map/all_gather | solution.py:35
  101.5 27.6 %while.10 = (s32[]{:T(128)}, f32[8,256]{1,0:T(8,128)S(1)}, bf16[8,256,256]{2,1,0:T(8,128)(2,1)S(1)}, f32[2048]{0:T(1024)S(1)}, bf16[2048,256]{1,0:T(8,128)(2,1)}...) while((s32[]{:T(128)}, f32[8,256]{1,0:T(8,128)S(1)}, bf16[8,256,256]{2,1,0:T(8,128)(2,1)S(1)}, ...), condition=%wide.region_4.5_spmd, body=%wide.region_1.4_spmd.sunk | while | flops 808910336 | bytes 3421289 | solution.py:45
  101.6 3.3 %fusion.33 = f32[256]{0:T(256)S(1)} fusion(bf16[2048,512]{1,0:T(8,128)(2,1)} %get-tuple-element.111, bf16[2048,256]{1,0:T(8,128)(2,1)} %get-tuple-element.110, f32[2048]{0:T(1024)S(1)} %get-tuple-element.109, f32[256]{0:T(256)S(1)} %multiply_reduce_fusion.5, bf16[8,256,256]{2,1,0:T(8,128)(2,1)S(1)} %get-tuple-element.108, s32[]{:T(128)S(6)} %copy.25), kind=kOutput, calls=%fused_computation.9.clone.1 | convolution fusion | flops 808713984 | bytes 3287044 | tf_op jit(solution)/shard_map/while/body/eval_jaxpr/dot_general | solution.py:42
  105.1 3.3 %fusion.33 = f32[256]{0:T(256)S(1)} fusion(bf16[2048,512]{1,0:T(8,128)(2,1)} %get-tuple-element.111, bf16[2048,256]{1,0:T(8,128)(2,1)} %get-tuple-element.110, f32[2048]{0:T(1024)S(1)} %get-tuple-element.109, f32[256]{0:T(256)S(1)} %multiply_reduce_fusion.5, bf16[8,256,256]{2,1,0:T(8,128)(2,1)S(1)} %get-tuple-element.108, s32[]{:T(128)S(6)} %copy.25), kind=kOutput, calls=%fused_computation.9.clone.1 | convolution fusion | flops 808713984 | bytes 3287044 | tf_op jit(solution)/shard_map/while/body/eval_jaxpr/dot_general | solution.py:42
  108.5 3.3 %fusion.33 = f32[256]{0:T(256)S(1)} fusion(bf16[2048,512]{1,0:T(8,128)(2,1)} %get-tuple-element.111, bf16[2048,256]{1,0:T(8,128)(2,1)} %get-tuple-element.110, f32[2048]{0:T(1024)S(1)} %get-tuple-element.109, f32[256]{0:T(256)S(1)} %multiply_reduce_fusion.5, bf16[8,256,256]{2,1,0:T(8,128)(2,1)S(1)} %get-tuple-element.108, s32[]{:T(128)S(6)} %copy.25), kind=kOutput, calls=%fused_computation.9.clone.1 | convolution fusion | flops 808713984 | bytes 3287044 | tf_op jit(solution)/shard_map/while/body/eval_jaxpr/dot_general | solution.py:42
  112.0 3.3 %fusion.33 = f32[256]{0:T(256)S(1)} fusion(bf16[2048,512]{1,0:T(8,128)(2,1)} %get-tuple-element.111, bf16[2048,256]{1,0:T(8,128)(2,1)} %get-tuple-element.110, f32[2048]{0:T(1024)S(1)} %get-tuple-element.109, f32[256]{0:T(256)S(1)} %multiply_reduce_fusion.5, bf16[8,256,256]{2,1,0:T(8,128)(2,1)S(1)} %get-tuple-element.108, s32[]{:T(128)S(6)} %copy.25), kind=kOutput, calls=%fused_computation.9.clone.1 | convolution fusion | flops 808713984 | bytes 3287044 | tf_op jit(solution)/shard_map/while/body/eval_jaxpr/dot_general | solution.py:42
  115.4 3.3 %fusion.33 = f32[256]{0:T(256)S(1)} fusion(bf16[2048,512]{1,0:T(8,128)(2,1)} %get-tuple-element.111, bf16[2048,256]{1,0:T(8,128)(2,1)} %get-tuple-element.110, f32[2048]{0:T(1024)S(1)} %get-tuple-element.109, f32[256]{0:T(256)S(1)} %multiply_reduce_fusion.5, bf16[8,256,256]{2,1,0:T(8,128)(2,1)S(1)} %get-tuple-element.108, s32[]{:T(128)S(6)} %copy.25), kind=kOutput, calls=%fused_computation.9.clone.1 | convolution fusion | flops 808713984 | bytes 3287044 | tf_op jit(solution)/shard_map/while/body/eval_jaxpr/dot_general | solution.py:42
  118.9 3.3 %fusion.33 = f32[256]{0:T(256)S(1)} fusion(bf16[2048,512]{1,0:T(8,128)(2,1)} %get-tuple-element.111, bf16[2048,256]{1,0:T(8,128)(2,1)} %get-tuple-element.110, f32[2048]{0:T(1024)S(1)} %get-tuple-element.109, f32[256]{0:T(256)S(1)} %multiply_reduce_fusion.5, bf16[8,256,256]{2,1,0:T(8,128)(2,1)S(1)} %get-tuple-element.108, s32[]{:T(128)S(6)} %copy.25), kind=kOutput, calls=%fused_computation.9.clone.1 | convolution fusion | flops 808713984 | bytes 3287044 | tf_op jit(solution)/shard_map/while/body/eval_jaxpr/dot_general | solution.py:42
  122.3 3.3 %fusion.33 = f32[256]{0:T(256)S(1)} fusion(bf16[2048,512]{1,0:T(8,128)(2,1)} %get-tuple-element.111, bf16[2048,256]{1,0:T(8,128)(2,1)} %get-tuple-element.110, f32[2048]{0:T(1024)S(1)} %get-tuple-element.109, f32[256]{0:T(256)S(1)} %multiply_reduce_fusion.5, bf16[8,256,256]{2,1,0:T(8,128)(2,1)S(1)} %get-tuple-element.108, s32[]{:T(128)S(6)} %copy.25), kind=kOutput, calls=%fused_computation.9.clone.1 | convolution fusion | flops 808713984 | bytes 3287044 | tf_op jit(solution)/shard_map/while/body/eval_jaxpr/dot_general | solution.py:42
  125.8 3.3 %fusion.33 = f32[256]{0:T(256)S(1)} fusion(bf16[2048,512]{1,0:T(8,128)(2,1)} %get-tuple-element.111, bf16[2048,256]{1,0:T(8,128)(2,1)} %get-tuple-element.110, f32[2048]{0:T(1024)S(1)} %get-tuple-element.109, f32[256]{0:T(256)S(1)} %multiply_reduce_fusion.5, bf16[8,256,256]{2,1,0:T(8,128)(2,1)S(1)} %get-tuple-element.108, s32[]{:T(128)S(6)} %copy.25), kind=kOutput, calls=%fused_computation.9.clone.1 | convolution fusion | flops 808713984 | bytes 3287044 | tf_op jit(solution)/shard_map/while/body/eval_jaxpr/dot_general | solution.py:42
  129.1 5.0 %all-reduce = f32[2048]{0:T(1024)S(1)} all-reduce(f32[2048]{0:T(1024)S(1)} %bitcast.52), channel_id=2, replica_groups=mesh['groups'=2,'rows'=4,'cols'=2,'sub'=2] {'cols'}, use_global_device_ids=true, to_apply=%region_5.6.clone | all-reduce | flops 2048 | bytes 16384
  134.1 2.5 %psum.7 = f32[1024]{0:T(1024)S(1)} all-reduce(f32[1024]{0:T(1024)S(1)} %dynamic-slice.1), channel_id=1, replica_groups=mesh['groups'=2,'rows'=4,'cols'=2,'sub'=2] {'sub'}, use_global_device_ids=true, to_apply=%region_6.7 | all-reduce | flops 1024 | bytes 8192 | tf_op jit(solution)/shard_map/psum | solution.py:47
  136.6 0.6 subtract_multiply_fusion
  (70 shorter events, 4.0 us)
Async XLA Ops:
  7.2 7.4 %copy-start.2 = (s32[1024,1]{0,1:T(1,128)S(1)}, s32[1024,1]{0,1:T(1,128)}, u32[]{:S(2)}) copy-start(s32[1024,1]{0,1:T(1,128)} %param.10) | copy-start | bytes 12292
  7.2 9.7 %copy-start.3 = (s32[1024]{0:T(1024)S(1)}, s32[1024]{0:T(1024)}, u32[]{:S(2)}) copy-start(s32[1024]{0:T(1024)} %param.11) | copy-start | bytes 12292
  7.2 16.7 %copy-start = (bf16[2048,256]{1,0:T(8,128)(2,1)S(1)}, bf16[2048,256]{1,0:T(8,128)(2,1)}, u32[]{:S(2)}) copy-start(bf16[2048,256]{1,0:T(8,128)(2,1)} %param.7) | copy-start | bytes 3145732
  7.2 58.8 %all-gather.3.cloned.1.call-start = ((), (), s32[]{:S(2)}) async-start(), calls=%async_computation.2 | async-start | bytes 1179648 | tf_op jit(solution)/shard_map/all_gather | solution.py:33
  9.8 13.0 %all-to-all-start = ((bf16[256,2,512]{2,0,1:T(8,128)(2,1)}), bf16[256,2,512]{2,0,1:T(8,128)(2,1)S(1)}, u32[]{:S(2)}, u32[]{:S(2)}) async-start(bf16[256,2,512]{2,0,1:T(8,128)(2,1)} %bitcast.36), calls=%async_computation | async-start | bytes 1048576 | tf_op jit(solution)/shard_map/all_to_all | solution.py:34
  14.0 87.5 %all-gather.5.cloned.1.call-start = ((), (), s32[]{:S(2)}) async-start(), calls=%async_computation.3 | async-start | bytes 2621440 | tf_op jit(solution)/shard_map/all_gather | solution.py:35
  22.8 0.8 copy-start.1
  23.6 35.9 %copy-start.4 = (u32[32]{0:T(128)S(1)}, u32[32]{0:T(128)}, u32[]{:S(2)}) copy-start(u32[32]{0:T(128)} %constant.126) | copy-start | bytes 388
  26.1 11.0 %all-to-all-start.1 = ((bf16[4,64,256]{2,1,0:T(8,128)(2,1)}), bf16[4,64,256]{2,1,0:T(8,128)(2,1)S(1)}, u32[]{:S(2)}, u32[]{:S(2)}) async-start(bf16[4,64,256]{2,1,0:T(8,128)(2,1)} %select_select_fusion), calls=%async_computation.1 | async-start | bytes 262144 | tf_op jit(solution)/shard_map/all_to_all | solution.py:66
  48.1 5.8 %collective-permute-start = (bf16[32,256]{1,0:T(8,128)(2,1)S(1)}, bf16[32,256]{1,0:T(8,128)(2,1)S(1)}, u32[]{:S(2)}, u32[]{:S(2)}) collective-permute-start(bf16[32,256]{1,0:T(8,128)(2,1)S(1)} %constant_dynamic-slice_fusion), channel_id=1, source_target_pairs={{0,4},{4,8},{8,12},{12,0},{1,5},{5,9},{9,13},{13,1},{2,6},{6,10},{... | collective-permute-start | bytes 49160 | tf_op jit(solution)/shard_map/ppermute | solution.py:78
  53.9 5.5 %collective-permute-start.1 = (bf16[32,256]{1,0:T(8,128)(2,1)S(1)}, bf16[32,256]{1,0:T(8,128)(2,1)S(1)}, u32[]{:S(2)}, u32[]{:S(2)}) collective-permute-start(bf16[32,256]{1,0:T(8,128)(2,1)S(1)} %collective-permute-done), channel_id=1, source_target_pairs={{0,4},{4,8},{8,12},{12,0},{1,5},{5,9},{9,13},{13,1},{2,6},{6,10},{... | collective-permute-start | bytes 49160 | tf_op jit(solution)/shard_map/ppermute | solution.py:78
  59.4 5.5 %collective-permute-start.2 = (bf16[32,256]{1,0:T(8,128)(2,1)S(1)}, bf16[32,256]{1,0:T(8,128)(2,1)S(1)}, u32[]{:S(2)}, u32[]{:S(2)}) collective-permute-start(bf16[32,256]{1,0:T(8,128)(2,1)S(1)} %collective-permute-done.1), channel_id=1, source_target_pairs={{0,4},{4,8},{8,12},{12,0},{1,5},{5,9},{9,13},{13,1},{2,6},{6,10},{... | collective-permute-start | bytes 49160 | tf_op jit(solution)/shard_map/ppermute | solution.py:78
Sparse Core Ops, SparseCore 0:
  10.1 43.8 all-gather.2
  55.6 45.8 all-gather.4
